TPU v7x, 32 devices: a whole 2x2x4 slice. The times are simulated.
32 devices in a mesh: group: 2 (over core), dp: 4 (over z), section: 2 (over x), tensor: 2 (over y).
Axes of the slice: x: 2, y: 2, z: 4, core: 2. Of those that a mesh axis runs over, the one named last changes fastest.
Arguments:
- merged: bfloat16 [768, 5120], P('dp'), may hold values from -6 to 6
- counts: int32 [8], P('dp'), may hold values from 4 to 384
- owners: int32 [768, 1], P('dp'), may hold values from 0 to 3; in each aligned block of 192 rows (0 to 191, 192 to 383, ...) at most 96 rows name the same one
- w_merge: bfloat16 [5120, 8192], P(None, ('group', 'section', 'tensor')), may hold values from -0.078125 to 0.078125
- norm_gain: float32 [8192], P(('group', 'section', 'tensor')), may hold values from 0.25 to 1.75
- cotangent: bfloat16 [4, 4, 96, 8192], P('dp', None, None, ('group', 'section', 'tensor')), may hold values from -6 to 6
Outputs:
- embedded: bfloat16 [4, 4, 96, 8192], P('dp', None, None, ('group', 'section', 'tensor'))
- grad_merged: float32 [768, 5120], P('dp', ('group', 'section', 'tensor'))
- grad_weight: float32 [5120, 8192], P('dp', ('group', 'section', 'tensor'))
Inputs may be any that keep to these rules, and one draw needn't show every extreme that they name: `owners`: in each replica's 192 rows no owner appears more than 96 times.
All inputs are finite; a program needn't handle non-finite values.
Results may differ from a plain program's by a relative error of at most 0.0049.
Values may be sent and summed in bfloat16 or wider, within the bound.
A program may use at most 64 MiB of HBM per device.

v0:
```python
import jax
import jax.numpy as jnp
from jax import lax
from jax.sharding import PartitionSpec as P

D = 8192


def on_device(merged, counts, owners, w_merge, norm_gain, cotangent):
    rows = merged.shape[0]
    columns = w_merge.shape[1]
    replicas = lax.axis_size("dp")
    slots = cotangent.shape[2]
    images = counts.shape[0]
    per_image = rows // images
    projected = jnp.dot(merged, w_merge, preferred_element_type=jnp.float32).astype(jnp.bfloat16)
    row_index = jnp.arange(rows, dtype=jnp.int32)
    image_of = row_index // per_image
    picked = image_of[:, None] == jnp.arange(images, dtype=jnp.int32)[None, :]
    count_of = jnp.sum(jnp.where(picked, counts[None, :], 0), axis=1)
    valid = (4 * (row_index % per_image) < count_of).astype(jnp.float32)
    masked = (projected.astype(jnp.float32) * valid[:, None]).astype(jnp.bfloat16)
    owner = owners[:, 0]
    hits = (owner[:, None] == jnp.arange(replicas, dtype=jnp.int32)[None, :]).astype(jnp.int32)
    before = jnp.cumsum(hits, axis=0) - hits
    slot_index = jnp.sum(before * hits, axis=1)
    target = owner * slots + slot_index
    placer = (jnp.arange(replicas * slots, dtype=jnp.int32)[:, None] == target[None, :]).astype(
        jnp.bfloat16
    )
    outgoing = jnp.dot(placer, masked, preferred_element_type=jnp.float32).astype(jnp.bfloat16)
    outgoing = outgoing.reshape(replicas, slots, columns)
    received = lax.all_to_all(outgoing, "dp", split_axis=0, concat_axis=0, tiled=True)
    values = received.astype(jnp.float32)
    square_sums = lax.psum(jnp.sum(values * values, axis=2), ("group", "section", "tensor"))
    scale = lax.rsqrt(square_sums / D + 1e-05)
    normed = (values * scale[:, :, None] * norm_gain[None, None, :]).astype(jnp.bfloat16)
    embedded = normed[None]
    grad_in = cotangent[0].astype(jnp.float32) * norm_gain[None, None, :]
    inner_sums = lax.psum(jnp.sum(grad_in * values, axis=2), ("group", "section", "tensor"))
    inner = inner_sums / D
    slot_grad = (scale[:, :, None] * grad_in - values * (scale**3 * inner)[:, :, None]).astype(
        jnp.bfloat16
    )
    returned = lax.all_to_all(slot_grad, "dp", split_axis=0, concat_axis=0, tiled=True)
    returned = returned.reshape(replicas * slots, columns)
    gathered = lax.dot_general(
        placer, returned, (((0,), (0,)), ((), ())), preferred_element_type=jnp.float32
    )
    back = (gathered * valid[:, None]).astype(jnp.bfloat16)
    input_terms = lax.dot_general(
        back, w_merge, (((1,), (1,)), ((), ())), preferred_element_type=jnp.float32
    )
    grad_merged = lax.psum_scatter(
        input_terms, ("group", "section", "tensor"), scatter_dimension=1, tiled=True
    )
    column_block = lax.all_to_all(merged, "dp", split_axis=1, concat_axis=0, tiled=True)
    grad_weight = lax.dot_general(
        column_block,
        lax.all_gather(back, "dp", axis=0, tiled=True),
        (((0,), (0,)), ((), ())),
        preferred_element_type=jnp.float32,
    )
    return (embedded, grad_merged, grad_weight)


def solution(mesh):
    placed = (
        P("dp", None),
        P("dp"),
        P("dp", None),
        P(None, ("group", "section", "tensor")),
        P(("group", "section", "tensor")),
        P("dp", None, None, ("group", "section", "tensor")),
    )
    return jax.shard_map(
        on_device,
        mesh=mesh,
        in_specs=placed,
        out_specs=(
            P("dp", None, None, ("group", "section", "tensor")),
            P("dp", ("group", "section", "tensor")),
            P("dp", ("group", "section", "tensor")),
        ),
        check_vma=False,
    )
```

profile of v0, /device:TPU:0, one launch (start us, length us, event | category | flops | bytes accessed | tf_op | source)
XLA Modules:
  0.0 182.4 jit_solution(6930971145670902794)
XLA Ops:
  8.0 0.0 all-gather.2.cloned.1.call-start
  8.1 0.7 iota_compare_fusion.3
  8.7 0.7 fusion.18
  9.5 1.2 reduce-window.6
  10.8 0.1 slice.12
  10.8 0.1 copy.23
  11.0 0.1 copy.24
  11.1 0.1 add_bitcast_fusion
  11.2 0.7 fusion.16
  11.9 0.7 multiply_add_fusion
  12.5 7.0 %convolution_convert_fusion = bf16[384,1024]{1,0:T(8,128)(2,1)S(1)} fusion(bf16[192,5120]{1,0:T(8,128)(2,1)} %param.6, bf16[5120,1024]{1,0:T(8,128)(2,1)} %param.9, f32[192]{0:T(256)S(1)} %compare_convert_fusion, s32[192]{0:T(256)S(1)} %multiply_add_fusion), kind=kOutput, calls=%fused_computation.14 | convolution fusion | flops 2165514240 | bytes 13239808 | tf_op jit(solution)/shard_map/dot_general | solution.py:31
  19.6 26.4 %all_to_all.29 = bf16[4,96,1024]{2,1,0:T(8,128)(2,1)S(1)} all-to-all(bf16[4,96,1024]{2,1,0:T(8,128)(2,1)S(1)} %bitcast.38), channel_id=1, replica_groups=mesh['group'=2,'dp'=4,'section'=2,'tensor'=2] {'dp'}, dimensions={0} | all-to-all | bytes 1572864 | tf_op jit(solution)/shard_map/all_to_all | solution.py:33
  46.0 0.4 fusion.3
  46.4 14.3 %all-reduce.1 = (f32[4,96]{1,0:T(4,128)S(1)}, f32[4,96]{1,0:T(4,128)S(1)}) all-reduce(f32[4,96]{1,0:T(4,128)S(1)} %get-tuple-element.19, f32[4,96]{1,0:T(4,128)S(1)} %get-tuple-element.18), channel_id=1, replica_groups=mesh['group'=2,'dp'=4,'section'=2,'tensor'=2] {'group','section','tensor'}, use_global_device_ids=true, to_apply=%region_5.6 | all-reduce | flops 768 | bytes 6144 | tf_op jit(solution)/shard_map/psum | solution.py:35
  60.7 1.4 fusion.5
  62.1 23.6 %all_to_all.30 = bf16[4,96,1024]{2,1,0:T(8,128)(2,1)S(1)} all-to-all(bf16[4,96,1024]{2,1,0:T(8,128)(2,1)S(1)} %get-tuple-element.22), channel_id=1, replica_groups=mesh['group'=2,'dp'=4,'section'=2,'tensor'=2] {'dp'}, dimensions={0} | all-to-all | bytes 1572864 | tf_op jit(solution)/shard_map/all_to_all | solution.py:45
  85.7 1.2 fusion.7
  86.9 0.0 reduce-scatter.2.cloned.1.call-start
  86.9 9.7 %fusion.21 = f32[192,5120]{1,0:T(8,128)} fusion(bf16[192,1024]{1,0:T(8,128)(2,1)} %fusion.7, bf16[5120,1024]{1,0:T(8,128)(2,1)} %param.9), kind=kOutput, calls=%fused_computation.48 | convolution fusion | flops 2013265920 | bytes 14811136 | tf_op jit(solution)/shard_map/dot_general | solution.py:51
  96.7 1.5 copy-done.1
  98.2 0.1 copy.31
  98.3 64.7 %all_to_all.31 = bf16[192,4,1280]{2,0,1:T(8,128)(2,1)S(1)} all-to-all(bf16[192,4,1280]{2,0,1:T(8,128)(2,1)S(1)} %bitcast.34), channel_id=1, replica_groups=mesh['group'=2,'dp'=4,'section'=2,'tensor'=2] {'dp'}, dimensions={1} | all-to-all | bytes 3932160 | tf_op jit(solution)/shard_map/all_to_all | solution.py:57
  163.1 6.0 %convolution_bitcast_fusion = f32[1280,1024]{0,1:T(8,128)} fusion(bf16[768,1024]{1,0:T(8,128)(2,1)} %all-gather.2.cloned.1.call-done, bf16[768,1280]{1,0:T(8,128)(2,1)S(1)} %bitcast.37), kind=kOutput, calls=%fused_computation | convolution fusion | flops 2013265920 | bytes 8781824 | tf_op jit(solution)/shard_map/dot_general | solution.py:58
  169.1 5.9 %copy.26 = f32[1280,1024]{1,0:T(8,128)} copy(f32[1280,1024]{0,1:T(8,128)} %convolution_bitcast_fusion) | data formatting | bytes 10485760
  (17 shorter events, 0.2 us)
Async XLA Ops:
  8.0 155.1 %all-gather.2.cloned.1.call-start = ((), (), s32[]{:S(2)}) async-start(), calls=%async_computation.5 | async-start | bytes 1966080 | tf_op jit(solution)/shard_map/all_gather | solution.py:60
  12.5 33.4 %copy-start.2 = (f32[1024]{0:T(1024)S(1)}, f32[1024]{0:T(1024)}, u32[]{:S(2)}) copy-start(f32[1024]{0:T(1024)} %param.10) | copy-start | bytes 12292
  19.6 26.4 %copy-start = (bf16[1,4,96,1024]{3,2,1,0:T(8,128)(2,1)S(1)}, bf16[1,4,96,1024]{3,2,1,0:T(8,128)(2,1)}, u32[]{:S(2)}) copy-start(bf16[1,4,96,1024]{3,2,1,0:T(8,128)(2,1)} %param.11) | copy-start | bytes 2359300
  86.9 88.1 %reduce-scatter.2.cloned.1.call-start = ((), (), s32[]{:S(2)}) async-start(), calls=%async_computation.4 | async-start | bytes 4423680 | tf_op jit(solution)/shard_map/reduce_scatter | solution.py:54
  96.7 1.5 copy-start.1
Sparse Core Ops, SparseCore 0:
  87.0 58.4 all-gather.1
Sparse Core Ops, SparseCore 1:
  96.8 46.7 reduce-scatter.1
where the time goes:
time: 183 us; the launch traced here: 182 us
  blocking collectives  129 us (70%)
  matrix products  23.9 us (13%)
  between operations  15.5 us (8%)
  local copies, waits for them, and re-layouts  7.84 us (4%)
  other arithmetic  6.04 us (3%)
    all_to_all x1, blocking collectives, on_device(): lax.all_to_all(merged, 'dp', split_axis=1, concat_axis=0, tiled=True)  64.7 us
    all_to_all x1, blocking collectives, on_device(): lax.all_to_all(outgoing, 'dp', split_axis=0, concat_axis=0, tiled=True)  26.4 us
    all_to_all x1, blocking collectives, on_device(): lax.all_to_all(slot_grad, 'dp', split_axis=0, concat_axis=0, tiled=True)  23.6 us
    psum x1, blocking collectives, on_device(): lax.psum(jnp.sum(values * values, axis=2), ('group', 'section', 'tensor'))  14.3 us
    dot_general x1, matrix products, on_device(): lax.dot_general(back, w_merge, (((1,), (1,)), ((), ())), preferred_elemen...  9.72 us
    unnamed x8, local copies, waits for them, and re-layouts  7.42 us
    dot_general x1, matrix products, on_device(): jnp.dot(placer, masked, preferred_element_type=jnp.float32)  7.02 us
    dot_general x1, matrix products, on_device(): lax.dot_general(column_block, lax.all_gather(back, 'dp', axis=0, tiled=Tr...  5.97 us
  transfers between devices with their start and end apart: 2, of which 0 were waited for; matrix products, arithmetic and copies ran while one was open for 12% of the time, Pallas kernels for 0%

commit v1 on v0

--- a/solution.py
+++ b/solution.py
@@ -4,6 +4,12 @@
 from jax.sharding import PartitionSpec as P
 
 D = 8192
+
+
+def trade_parts(shard, axis, split, join):
+    pieces = jnp.split(shard, lax.axis_size(axis), axis=split)
+    incoming = lax.all_to_all(jnp.stack(pieces), axis, 0, 0)
+    return jnp.concatenate(incoming, axis=join)
 
 
 def on_device(merged, counts, owners, w_merge, norm_gain, cotangent):
@@ -54,7 +60,7 @@
     grad_merged = lax.psum_scatter(
         input_terms, ("group", "section", "tensor"), scatter_dimension=1, tiled=True
     )
-    column_block = lax.all_to_all(merged, "dp", split_axis=1, concat_axis=0, tiled=True)
+    column_block = trade_parts(merged, "dp", 1, 0)
     grad_weight = lax.dot_general(
         column_block,
         lax.all_gather(back, "dp", axis=0, tiled=True),

time: 183 us -> 177 us (0.967)
  local copies, waits for them, and re-layouts: 7.84 us -> 1.96 us
    unnamed x8 -> x7, local copies, waits for them, and re-layouts: 7.42 us -> 1.54 us
  transfers between devices with their start and end apart: 2 -> 2, of which waited for: 0 -> 0; matrix products, arithmetic and copies ran while one was open for 12% -> 9% of each run, Pallas kernels for 0% -> 0%
where the time goes in v1:
time: 177 us
  blocking collectives  129 us (73%)
  matrix products  23.8 us (13%)
  between operations  15.5 us (9%)
  other arithmetic  6.29 us (4%)
  local copies, waits for them, and re-layouts  1.96 us (1%)
    all_to_all x1, blocking collectives, trade_parts(): incoming = lax.all_to_all(jnp.stack(pieces), axis, 0, 0)  64.6 us
    all_to_all x1, blocking collectives, on_device(): lax.all_to_all(outgoing, 'dp', split_axis=0, concat_axis=0, tiled=True)  26.4 us
    all_to_all x1, blocking collectives, on_device(): lax.all_to_all(slot_grad, 'dp', split_axis=0, concat_axis=0, tiled=True)  23.6 us
    psum x1, blocking collectives, on_device(): lax.psum(jnp.sum(values * values, axis=2), ('group', 'section', 'tensor'))  14.3 us
    dot_general x1, matrix products, on_device(): lax.dot_general(back, w_merge, (((1,), (1,)), ((), ())), preferred_elemen...  9.65 us
    dot_general x1, matrix products, on_device(): jnp.dot(placer, masked, preferred_element_type=jnp.float32)  7.02 us
    dot_general x1, matrix products, on_device(): lax.dot_general(column_block, lax.all_gather(back, 'dp', axis=0, tiled=Tr...  6.01 us
  transfers between devices with their start and end apart: 2, of which 0 were waited for; matrix products, arithmetic and copies ran while one was open for 9% of the time, Pallas kernels for 0%

profile of v1, /device:TPU:0, one launch (start us, length us, event | category | flops | bytes accessed | tf_op | source)
XLA Modules:
  0.0 176.5 jit_solution(17498395571306647157)
XLA Ops:
  8.0 0.0 all-gather.2.cloned.1.call-start
  8.1 0.7 fusion.18
  8.8 0.7 iota_compare_fusion.3
  9.5 1.2 reduce-window.6
  10.7 0.1 slice.12
  10.8 0.1 copy.11
  11.0 0.1 copy.12
  11.1 0.1 add_bitcast_fusion
  11.1 0.7 fusion.16
  11.8 0.7 multiply_add_fusion
  12.5 7.0 %convolution_convert_fusion = bf16[384,1024]{1,0:T(8,128)(2,1)S(1)} fusion(bf16[192,5120]{1,0:T(8,128)(2,1)} %param.6, bf16[5120,1024]{1,0:T(8,128)(2,1)} %param.9, f32[192]{0:T(256)S(1)} %compare_convert_fusion, s32[192]{0:T(256)S(1)} %multiply_add_fusion), kind=kOutput, calls=%fused_computation.13 | convolution fusion | flops 2165514240 | bytes 13239808 | tf_op jit(solution)/shard_map/dot_general | solution.py:37
  19.6 26.4 %all_to_all.15 = bf16[4,96,1024]{2,1,0:T(8,128)(2,1)S(1)} all-to-all(bf16[4,96,1024]{2,1,0:T(8,128)(2,1)S(1)} %bitcast.36), channel_id=1, replica_groups=mesh['group'=2,'dp'=4,'section'=2,'tensor'=2] {'dp'}, dimensions={0} | all-to-all | bytes 1572864 | tf_op jit(solution)/shard_map/all_to_all | solution.py:39
  46.0 0.4 fusion.3
  46.4 14.3 %all-reduce.1 = (f32[4,96]{1,0:T(4,128)S(1)}, f32[4,96]{1,0:T(4,128)S(1)}) all-reduce(f32[4,96]{1,0:T(4,128)S(1)} %get-tuple-element.4, f32[4,96]{1,0:T(4,128)S(1)} %get-tuple-element.3), channel_id=1, replica_groups=mesh['group'=2,'dp'=4,'section'=2,'tensor'=2] {'group','section','tensor'}, use_global_device_ids=true, to_apply=%region_5.6 | all-reduce | flops 768 | bytes 6144 | tf_op jit(solution)/shard_map/psum | solution.py:41
  60.7 1.4 fusion.5
  62.1 23.6 %all_to_all.16 = bf16[4,96,1024]{2,1,0:T(8,128)(2,1)S(1)} all-to-all(bf16[4,96,1024]{2,1,0:T(8,128)(2,1)S(1)} %get-tuple-element.11), channel_id=1, replica_groups=mesh['group'=2,'dp'=4,'section'=2,'tensor'=2] {'dp'}, dimensions={0} | all-to-all | bytes 1572864 | tf_op jit(solution)/shard_map/all_to_all | solution.py:51
  85.7 1.2 fusion.7
  86.9 0.0 reduce-scatter.2.cloned.1.call-start
  86.9 9.7 %fusion.21 = f32[192,5120]{1,0:T(8,128)} fusion(bf16[192,1024]{1,0:T(8,128)(2,1)} %fusion.7, bf16[5120,1024]{1,0:T(8,128)(2,1)} %param.9), kind=kOutput, calls=%fused_computation.51 | convolution fusion | flops 2013265920 | bytes 14811136 | tf_op jit(solution)/shard_map/dot_general | solution.py:57
  96.6 1.5 copy-done.1
  98.1 0.1 slice_bitcast_fusion.3
  98.3 0.2 pad_maximum_fusion
  98.5 64.6 %all_to_all.17 = bf16[4,192,1280]{2,1,0:T(8,128)(2,1)S(1)} all-to-all(bf16[4,192,1280]{2,1,0:T(8,128)(2,1)S(1)} %pad_maximum_fusion), channel_id=1, replica_groups=mesh['group'=2,'dp'=4,'section'=2,'tensor'=2] {'dp'}, dimensions={0} | all-to-all | bytes 3932160 | tf_op jit(solution)/shard_map/all_to_all | solution.py:11
  163.1 6.0 %fusion.22 = f32[1280,1024]{1,0:T(8,128)} fusion(bf16[768,1280]{1,0:T(8,128)(2,1)S(1)} %bitcast.35, bf16[768,1024]{1,0:T(8,128)(2,1)} %all-gather.2.cloned.1.call-done), kind=kOutput, calls=%fused_computation.52 | convolution fusion | flops 2013265920 | bytes 8781824 | tf_op jit(solution)/shard_map/dot_general | solution.py:64
  (17 shorter events, 0.2 us)
Async XLA Ops:
  8.0 155.1 %all-gather.2.cloned.1.call-start = ((), (), s32[]{:S(2)}) async-start(), calls=%async_computation.5 | async-start | bytes 1966080 | tf_op jit(solution)/shard_map/all_gather | solution.py:66
  12.5 33.4 %copy-start.2 = (f32[1024]{0:T(1024)S(1)}, f32[1024]{0:T(1024)}, u32[]{:S(2)}) copy-start(f32[1024]{0:T(1024)} %param.10) | copy-start | bytes 12292
  19.6 26.4 %copy-start = (bf16[1,4,96,1024]{3,2,1,0:T(8,128)(2,1)S(1)}, bf16[1,4,96,1024]{3,2,1,0:T(8,128)(2,1)}, u32[]{:S(2)}) copy-start(bf16[1,4,96,1024]{3,2,1,0:T(8,128)(2,1)} %param.11) | copy-start | bytes 2359300
  86.9 82.2 %reduce-scatter.2.cloned.1.call-start = ((), (), s32[]{:S(2)}) async-start(), calls=%async_computation.4 | async-start | bytes 4423680 | tf_op jit(solution)/shard_map/reduce_scatter | solution.py:60
  96.6 1.5 copy-start.1
Sparse Core Ops, SparseCore 0:
  87.0 58.3 all-gather.1
Sparse Core Ops, SparseCore 1:
  96.7 46.7 reduce-scatter.1
